TPU v7x, 32 devices: a whole 2x2x4 slice. The times are simulated.
32 devices in a mesh: seq: 8 (over y, x, core), head: 4 (over z).
Axes of the slice: x: 2, y: 2, z: 4, core: 2. Of those that a mesh axis runs over, the one named last changes fastest.
Arguments:
- queries: bfloat16 [2048, 4096], P(('seq', 'head')), may hold values from -10 to 10
- keys: bfloat16 [2048, 1024], P(('seq', 'head')), may hold values from -10 to 10
- block_pos: int32 [16], replicated, may hold values from 0 to 15, each once
- query_map: float32 [32, 128, 128], P('head'), may hold values from -4 to 4
- key_map: float32 [8, 128, 128], P('head'), may hold values from -4 to 4
Outputs:
- query_map_gradient: float32 [32, 128, 128], P('head')
- key_map_gradient: float32 [8, 128, 128], P('head')
Inputs may be any that keep to these rules, and one draw needn't show every extreme that they name: A permutation: stored block g (token rows g * 128 to (g + 1) * 128 - 1) holds position block block_pos[g]; position blocks below 8 form the first sequence, the others the second.
All inputs are finite; a program needn't handle non-finite values.
Results may differ from a plain program's by a relative error of at most 0.0021.
Values may be sent and summed in bfloat16 or wider, within the bound.
No kernel may reach another device: no remote copies, remote signals or barrier semaphores. Data moves between devices by JAX's collectives and lax.ppermute only.
A program may use at most 64 MiB of HBM per device.

v0:
```python
import math
import jax
import jax.numpy as jnp
from jax import lax
from jax.sharding import PartitionSpec as P

HEAD_SIZE = 128
BLK = 128
HIGHEST = lax.Precision.HIGHEST
NEG_FLOOR = -1e30


def softmax_pair(logits):
    return jnp.concatenate(
        [jax.nn.softmax(logits, axis=-1), jax.nn.softmax(-logits, axis=-1)], axis=-1
    )


def feature_grad(feature, upstream):
    half_width = feature.shape[-1] // 2
    positive, negative = (feature[..., :half_width], feature[..., half_width:])
    grad_positive, grad_negative = (upstream[..., :half_width], upstream[..., half_width:])
    first = positive * (grad_positive - jnp.sum(grad_positive * positive, axis=-1, keepdims=True))
    second = negative * (grad_negative - jnp.sum(grad_negative * negative, axis=-1, keepdims=True))
    return first - second


def row_places(row_index, block_pos, seq_count):
    stored = row_index // BLK
    lookup = stored[:, None] == jnp.arange(block_pos.shape[0], dtype=jnp.int32)[None, :]
    blocks = jnp.sum(jnp.where(lookup, block_pos[None, :], 0), axis=1)
    return (blocks // seq_count, blocks * BLK + row_index % BLK)


def over_blocks(running, portions, step_fn):
    row_count = portions[0].shape[1]
    step_rows = math.gcd(row_count, 512)

    def advance(number, inner_carry):
        slabs = tuple(
            (
                lax.dynamic_slice_in_dim(portion, number * step_rows, step_rows, 1)
                for portion in portions
            )
        )
        return step_fn(inner_carry, slabs, number * step_rows)

    return lax.fori_loop(0, row_count // step_rows, advance, running)


def per_device(queries, keys, block_pos, query_map, key_map):
    local_q, local_k = (
        lax.all_to_all(queries, "head", split_axis=1, concat_axis=0, tiled=True),
        lax.all_to_all(keys, "head", split_axis=1, concat_axis=0, tiled=True),
    )
    seq_count = lax.axis_size("seq")
    seq_rank = lax.axis_index("seq")
    rows_local = local_k.shape[0]
    token_count = rows_local * seq_count
    key_heads = key_map.shape[0]
    group_width = query_map.shape[0] // key_heads
    score_scale = HEAD_SIZE ** (-0.5)
    query_index = seq_rank * rows_local + jnp.arange(rows_local, dtype=jnp.int32)
    query_heads = local_q.reshape(rows_local, key_heads, group_width, HEAD_SIZE).transpose(
        1, 2, 0, 3
    )
    query_wide = query_heads.astype(jnp.float32)
    query_logits = jnp.einsum(
        "vgnd,vgde->vgne",
        query_wide,
        query_map.reshape(key_heads, group_width, HEAD_SIZE, HEAD_SIZE),
        precision=HIGHEST,
    )
    rows_all = group_width * rows_local
    phi_query = softmax_pair(query_logits).reshape(key_heads, rows_all, 2 * HEAD_SIZE)
    phi_query_b = phi_query.astype(jnp.bfloat16)
    query_flat = query_heads.reshape(key_heads, rows_all, HEAD_SIZE)
    query_seq, query_at = row_places(query_index, block_pos, seq_count)
    query_seq = jnp.tile(query_seq, group_width)
    query_at = jnp.tile(query_at, group_width)

    def visible_for(offset, slab_rows):
        key_index = offset + jnp.arange(slab_rows, dtype=jnp.int32)
        key_seq, key_at = row_places(key_index, block_pos, seq_count)
        return (key_seq[None, :] == query_seq[:, None]) & (key_at[None, :] <= query_at[:, None])

    def key_features(key_slab):
        logits = jnp.einsum(
            "vwd,vde->vwe", key_slab.astype(jnp.float32), key_map, precision=HIGHEST
        )
        return softmax_pair(logits)

    def teacher(key_slab):
        return (
            jnp.einsum("vrd,vwd->vrw", query_flat, key_slab, preferred_element_type=jnp.float32)
            * score_scale
        )

    def stats_step(running, slabs, offset):
        key_slab = slabs[0]
        visible = visible_for(offset, key_slab.shape[1])

        def stats_compute_live(current):
            highest, denominator, linear_sum = current
            masked = jnp.where(visible[None], teacher(key_slab), NEG_FLOOR)
            new_high = jnp.maximum(highest, jnp.max(masked, axis=-1))
            exponent = jnp.where(visible[None], jnp.exp(masked - new_high[..., None]), 0.0)
            denominator = denominator * jnp.exp(highest - new_high) + jnp.sum(exponent, axis=-1)
            phi_key_b = key_features(key_slab).astype(jnp.bfloat16)
            linear = jnp.einsum(
                "vrf,vwf->vrw", phi_query_b, phi_key_b, preferred_element_type=jnp.float32
            )
            linear_sum = linear_sum + jnp.sum(jnp.where(visible[None], linear, 0.0), axis=-1)
            return (new_high, denominator, linear_sum)

        return lax.cond(jnp.any(visible), stats_compute_live, lambda current: current, running)

    def grads_step(running, slabs, offset):
        key_slab = slabs[0]
        visible = visible_for(offset, key_slab.shape[1])

        def grads_compute_live(current):
            query_grad, key_weight_grad = current
            masked = jnp.where(visible[None], teacher(key_slab), NEG_FLOOR)
            exponent = jnp.where(visible[None], jnp.exp(masked - highest[..., None]), 0.0)
            teacher_prob = exponent / denominator[..., None]
            phi_key = key_features(key_slab)
            phi_key_b = phi_key.astype(jnp.bfloat16)
            linear = jnp.einsum(
                "vrf,vwf->vrw", phi_query_b, phi_key_b, preferred_element_type=jnp.float32
            )
            weights = (
                jnp.where(visible[None], 1.0 / linear_sum[..., None] - teacher_prob / linear, 0.0)
                / token_count
            ).astype(jnp.bfloat16)
            query_grad = query_grad + jnp.einsum(
                "vrw,vwf->vrf", weights, phi_key_b, preferred_element_type=jnp.float32
            )
            key_grad = jnp.einsum(
                "vrw,vrf->vwf", weights, phi_query_b, preferred_element_type=jnp.float32
            )
            key_logit_grad = feature_grad(phi_key, key_grad)
            key_weight_grad = key_weight_grad + jnp.einsum(
                "vwd,vwe->vde", key_slab.astype(jnp.float32), key_logit_grad, precision=HIGHEST
            )
            return (query_grad, key_weight_grad)

        return lax.cond(jnp.any(visible), grads_compute_live, lambda current: current, running)

    def as_heads(pieces):
        return pieces.reshape(pieces.shape[0], key_heads, -1).transpose(1, 0, 2)

    row_zeros = jnp.zeros((key_heads, rows_all), jnp.float32)
    stats_init = (jnp.full((key_heads, rows_all), NEG_FLOOR, jnp.float32), row_zeros, row_zeros)
    grads_init = (
        jnp.zeros((key_heads, rows_all, 2 * HEAD_SIZE), jnp.float32),
        jnp.zeros((key_heads, HEAD_SIZE, HEAD_SIZE), jnp.float32),
    )
    highest, denominator, linear_sum = over_blocks(
        stats_init, (as_heads(lax.all_gather(local_k, "seq", axis=0, tiled=True)),), stats_step
    )
    query_grad, key_weight_grad = over_blocks(
        grads_init, (as_heads(lax.all_gather(local_k, "seq", axis=0, tiled=True)),), grads_step
    )
    query_logit_grad = feature_grad(phi_query, query_grad).reshape(
        key_heads, group_width, rows_local, HEAD_SIZE
    )
    query_weight_grad = jnp.einsum(
        "vgnd,vgne->vgde", query_wide, query_logit_grad, precision=HIGHEST
    ).reshape(key_heads * group_width, HEAD_SIZE, HEAD_SIZE)
    query_map_gradient, key_map_gradient = lax.psum((query_weight_grad, key_weight_grad), "seq")
    return (query_map_gradient, key_map_gradient)


def solution(mesh):
    in_specs = (
        P(("seq", "head"), None),
        P(("seq", "head"), None),
        P(),
        P("head", None, None),
        P("head", None, None),
    )
    out_specs = (P("head", None, None), P("head", None, None))
    return jax.shard_map(
        per_device, mesh=mesh, in_specs=in_specs, out_specs=out_specs, check_vma=False
    )
```

profile of v0, /device:TPU:0, one launch (start us, length us, event | category | flops | bytes accessed | tf_op | source)
XLA Modules:
  0.0 218.9 jit_solution(3189689803761205006)
XLA Ops:
  7.2 1.6 copy.131
  8.8 6.3 %all-to-all-start.1 = ((bf16[64,4,256]{2,0,1:T(8,128)(2,1)}), bf16[64,4,256]{2,0,1:T(8,128)(2,1)S(1)}, u32[]{:S(2)}, u32[]{:S(2)}) async-start(bf16[64,4,256]{2,0,1:T(8,128)(2,1)} %bitcast.86), calls=%async_computation.1 | async-start | bytes 262144 | tf_op jit(solution)/shard_map/all_to_all | solution.py:54
  15.2 1.9 copy.130
  17.0 4.2 %all-to-all-done.1 = bf16[64,4,256]{2,0,1:T(8,128)(2,1)S(1)} async-done(((bf16[64,4,256]{2,0,1:T(8,128)(2,1)}), bf16[64,4,256]{2,0,1:T(8,128)(2,1)S(1)}, u32[]{:S(2)}, u32[]{:S(2)}) %all-to-all-start.1) | async-done | bytes 131104 | tf_op jit(solution)/shard_map/all_to_all | solution.py:54
  21.2 3.5 %all-to-all-start = ((bf16[64,4,1024]{2,0,1:T(8,128)(2,1)}), bf16[64,4,1024]{2,0,1:T(8,128)(2,1)S(1)}, u32[]{:S(2)}, u32[]{:S(2)}) async-start(bf16[64,4,1024]{2,0,1:T(8,128)(2,1)} %bitcast.85), calls=%async_computation | async-start | bytes 1048576 | tf_op jit(solution)/shard_map/all_to_all | solution.py:53
  27.3 10.6 %all-to-all-done = bf16[64,4,1024]{2,0,1:T(8,128)(2,1)S(1)} async-done(((bf16[64,4,1024]{2,0,1:T(8,128)(2,1)}), bf16[64,4,1024]{2,0,1:T(8,128)(2,1)S(1)}, u32[]{:S(2)}, u32[]{:S(2)}) %all-to-all-start) | async-done | bytes 524320 | tf_op jit(solution)/shard_map/all_to_all | solution.py:53
  41.6 3.0 %pad_maximum_fusion.3 = f32[2,4,256,256]{2,3,1,0:T(8,128)} fusion(f32[2,4,256,128]{2,3,1,0:T(8,128)} %fusion.93, f32[2,4,256,128]{2,3,1,0:T(8,128)} %fusion.95), kind=kLoop, calls=%fused_computation.126 | loop fusion | flops 524288 | bytes 4194304 | tf_op jit(solution)/shard_map/concatenate | solution.py:14
  44.6 1.9 copy.94
  47.8 2.3 %copy.101 = bf16[2,1024,256]{1,2,0:T(8,128)(2,1)} copy(bf16[2,1024,256]{2,1,0:T(8,128)(2,1)} %bitcast_convert_fusion) | data formatting | bytes 2097152
  50.0 2.8 %all-gather.2.cloned.1.call-done = bf16[2048,256]{1,0:T(8,128)(2,1)} async-done(((bf16[256,256]{1,0:T(8,128)(2,1)}), bf16[2048,256]{1,0:T(8,128)(2,1)}) %all-gather.2.cloned.1.call-update) | async-done | bytes 1048592 | tf_op jit(solution)/shard_map/all_gather | solution.py:163
  52.8 2.3 %copy.96 = bf16[2048,256]{0,1:T(8,128)(2,1)} copy(bf16[2048,256]{1,0:T(8,128)(2,1)} %all-gather.2.cloned.1.call-done) | data formatting | bytes 2097152 | tf_op jit(solution)/shard_map/all_gather | solution.py:163
  55.1 2.3 %copy.97 = bf16[2,2048,128]{2,1,0:T(8,128)(2,1)} copy(bf16[2,2048,128]{1,2,0:T(8,128)(2,1)} %bitcast.103) | data formatting | bytes 2097152
  57.4 28.7 %while.40 = (s32[]{:T(128)}, f32[2,1024]{1,0:T(2,128)S(1)}, f32[2,1024]{1,0:T(2,128)S(1)}, f32[2,1024]{1,0:T(2,128)S(1)}, s32[16]{0:T(128)S(1)}, /*index=5*/bf16...) while((s32[]{:T(128)}, f32[2,1024]{1,0:T(2,128)S(1)}, ...), condition=%wide.region_17.18_spmd.clone, body=%wide.region_5.17_spmd.clone.sunk | while | flops 1021495552 | bytes 21834140 | solution.py:48
  59.5 6.8 %conditional.6 = ((f32[2,1024]{1,0:T(2,128)S(1)}, f32[2,1024]{1,0:T(2,128)S(1)}, f32[2,1024]{1,0:T(2,128)S(1)})) conditional(s32[]{:T(128)} %convert_element_type.44, (f32[2,1024]{1,0:T(2,128)S(1)}, f32[2,1024]{1,0:T(2,128)S(1)}, f32[2,1024]{1,0:T(2,128)S(1)}) %tuple.150, (pred[1024,512]{0,1:T(8,128)(4,1)S(1)}, s32[]{:T(128)}, ...), branch_computations={%region_8.8_spmd, %region_9.16_spmd} | conditional | flops 1019351296 | bytes 21258342 | solution.py:116
  59.5 1.4 fusion.20
  63.1 2.0 fusion.11
  68.4 6.8 %conditional.6 = ((f32[2,1024]{1,0:T(2,128)S(1)}, f32[2,1024]{1,0:T(2,128)S(1)}, f32[2,1024]{1,0:T(2,128)S(1)})) conditional(s32[]{:T(128)} %convert_element_type.44, (f32[2,1024]{1,0:T(2,128)S(1)}, f32[2,1024]{1,0:T(2,128)S(1)}, f32[2,1024]{1,0:T(2,128)S(1)}) %tuple.150, (pred[1024,512]{0,1:T(8,128)(4,1)S(1)}, s32[]{:T(128)}, ...), branch_computations={%region_8.8_spmd, %region_9.16_spmd} | conditional | flops 1019351296 | bytes 21258342 | solution.py:116
  68.4 1.4 fusion.20
  72.0 2.0 fusion.11
  77.2 6.8 %conditional.6 = ((f32[2,1024]{1,0:T(2,128)S(1)}, f32[2,1024]{1,0:T(2,128)S(1)}, f32[2,1024]{1,0:T(2,128)S(1)})) conditional(s32[]{:T(128)} %convert_element_type.44, (f32[2,1024]{1,0:T(2,128)S(1)}, f32[2,1024]{1,0:T(2,128)S(1)}, f32[2,1024]{1,0:T(2,128)S(1)}) %tuple.150, (pred[1024,512]{0,1:T(8,128)(4,1)S(1)}, s32[]{:T(128)}, ...), branch_computations={%region_8.8_spmd, %region_9.16_spmd} | conditional | flops 1019351296 | bytes 21258342 | solution.py:116
  77.3 1.4 fusion.20
  80.9 2.0 fusion.11
  86.3 43.1 %while.41 = (s32[]{:T(128)}, f32[2,1024,256]{2,1,0:T(8,128)S(1)}, f32[2,128,128]{2,1,0:T(8,128)S(1)}, s32[16]{0:T(128)S(1)}, f32[2,1024]{1,0:T(2,128)S(1)}, /*in...) while((s32[]{:T(128)}, f32[2,1024,256]{2,1,0:T(8,128)S(1)}, ...), condition=%wide.region_29.30_spmd.clone, body=%wide.region_18.29_spmd.clone.sunk | while | flops 2299869440 | bytes 40643016 | solution.py:48
  86.5 1.9 fusion.130
  89.0 10.8 %conditional.7 = ((f32[2,1024,256]{2,1,0:T(8,128)S(1)}, f32[2,128,128]{2,1,0:T(8,128)S(1)})) conditional(s32[]{:T(128)} %convert_element_type.45, (f32[2,1024,256]{2,1,0:T(8,128)S(1)}, f32[2,128,128]{2,1,0:T(8,128)S(1)}) %tuple.156, (pred[1024,512]{0,1:T(8,128)(4,1)}, f32[2,1024]{1,0:T(2,128)S(1)}, s32[]{:T(128)}, ...), branch_computations={%region_21.21_spmd, %region_22.28_spmd} | conditional | flops 2297725184 | bytes 40067196 | solution.py:148
  89.0 1.3 fusion.51
  91.5 1.7 fusion.53
  93.2 2.5 %fusion.35 = bf16[2,1024,512]{1,2,0:T(8,128)(2,1)S(1)} fusion(f32[2,512,1024]{2,1,0:T(8,128)S(1)} %fusion.53, bf16[2,1024,256]{1,2,0:T(8,128)(2,1)S(1)} %copy-done.1, f32[2,1024]{1,0:T(2,128)S(1)} %get-tuple-element.811, f32[2,1024]{1,0:T(2,128)S(1)} %get-tuple-element.810, f32[2,1024]{1,0:T(2,128)S(1)} %broadcast_divide_fusion.2, ...), kind=kOutput, calls=%fused_computation.40 | convolution fusion | flops 548405248 | bytes 8413184 | tf_op jit(solution)/shard_map/while/body/eval_jaxpr/cond/branch_1_fun/vrf,vwf->vrw/dot_general | solution.py:129
  96.5 1.4 convolution_add_fusion
  98.2 1.6 convolution_add_fusion.1
  99.9 1.9 fusion.130
  102.4 10.8 %conditional.7 = ((f32[2,1024,256]{2,1,0:T(8,128)S(1)}, f32[2,128,128]{2,1,0:T(8,128)S(1)})) conditional(s32[]{:T(128)} %convert_element_type.45, (f32[2,1024,256]{2,1,0:T(8,128)S(1)}, f32[2,128,128]{2,1,0:T(8,128)S(1)}) %tuple.156, (pred[1024,512]{0,1:T(8,128)(4,1)}, f32[2,1024]{1,0:T(2,128)S(1)}, s32[]{:T(128)}, ...), branch_computations={%region_21.21_spmd, %region_22.28_spmd} | conditional | flops 2297725184 | bytes 40067196 | solution.py:148
  105.0 1.7 fusion.53
  106.7 2.5 %fusion.35 = bf16[2,1024,512]{1,2,0:T(8,128)(2,1)S(1)} fusion(f32[2,512,1024]{2,1,0:T(8,128)S(1)} %fusion.53, bf16[2,1024,256]{1,2,0:T(8,128)(2,1)S(1)} %copy-done.1, f32[2,1024]{1,0:T(2,128)S(1)} %get-tuple-element.811, f32[2,1024]{1,0:T(2,128)S(1)} %get-tuple-element.810, f32[2,1024]{1,0:T(2,128)S(1)} %broadcast_divide_fusion.2, ...), kind=kOutput, calls=%fused_computation.40 | convolution fusion | flops 548405248 | bytes 8413184 | tf_op jit(solution)/shard_map/while/body/eval_jaxpr/cond/branch_1_fun/vrf,vwf->vrw/dot_general | solution.py:129
  109.9 1.4 convolution_add_fusion
  111.6 1.6 convolution_add_fusion.1
  113.4 1.9 fusion.130
  115.9 10.8 %conditional.7 = ((f32[2,1024,256]{2,1,0:T(8,128)S(1)}, f32[2,128,128]{2,1,0:T(8,128)S(1)})) conditional(s32[]{:T(128)} %convert_element_type.45, (f32[2,1024,256]{2,1,0:T(8,128)S(1)}, f32[2,128,128]{2,1,0:T(8,128)S(1)}) %tuple.156, (pred[1024,512]{0,1:T(8,128)(4,1)}, f32[2,1024]{1,0:T(2,128)S(1)}, s32[]{:T(128)}, ...), branch_computations={%region_21.21_spmd, %region_22.28_spmd} | conditional | flops 2297725184 | bytes 40067196 | solution.py:148
  118.5 1.7 fusion.53
  120.1 2.5 %fusion.35 = bf16[2,1024,512]{1,2,0:T(8,128)(2,1)S(1)} fusion(f32[2,512,1024]{2,1,0:T(8,128)S(1)} %fusion.53, bf16[2,1024,256]{1,2,0:T(8,128)(2,1)S(1)} %copy-done.1, f32[2,1024]{1,0:T(2,128)S(1)} %get-tuple-element.811, f32[2,1024]{1,0:T(2,128)S(1)} %get-tuple-element.810, f32[2,1024]{1,0:T(2,128)S(1)} %broadcast_divide_fusion.2, ...), kind=kOutput, calls=%fused_computation.40 | convolution fusion | flops 548405248 | bytes 8413184 | tf_op jit(solution)/shard_map/while/body/eval_jaxpr/cond/branch_1_fun/vrf,vwf->vrw/dot_general | solution.py:129
  123.4 1.4 convolution_add_fusion
  125.1 1.6 convolution_add_fusion.1
  126.8 1.9 fusion.130
  129.4 2.0 fusion.86
  131.4 2.1 fusion.84
  135.6 73.0 %all-reduce.3.cloned.1.call-done = (f32[8,128,128]{2,1,0:T(8,128)}, f32[2,128,128]{2,1,0:T(8,128)}) async-done(((f32[8,128,128]{2,1,0:T(8,128)}, f32[2,128,128]{2,1,0:T(8,128)}), (f32[8,128,128]{2,1,0:T(8,128)}, f32[2,128,128]{2,1,0:T(8,128)})) %all-reduce.3.cloned.1.call-update) | async-done | bytes 655376 | tf_op jit(solution)/shard_map/psum | solution.py:171
  208.6 1.9 copy.175
  210.5 1.6 copy.176
  (154 shorter events, 34.8 us)
Async XLA Ops:
  7.2 31.2 %copy-start = (f32[8,128,128]{2,1,0:T(8,128)S(1)}, f32[8,128,128]{2,1,0:T(8,128)}, u32[]{:S(2)}) copy-start(f32[8,128,128]{2,1,0:T(8,128)} %param.16) | copy-start | bytes 1572868
  8.8 12.4 %all-to-all-start.1 = ((bf16[64,4,256]{2,0,1:T(8,128)(2,1)}), bf16[64,4,256]{2,0,1:T(8,128)(2,1)S(1)}, u32[]{:S(2)}, u32[]{:S(2)}) async-start(bf16[64,4,256]{2,0,1:T(8,128)(2,1)} %bitcast.86), calls=%async_computation.1 | async-start | bytes 262144 | tf_op jit(solution)/shard_map/all_to_all | solution.py:54
  21.2 3.5 %copy-start.8 = (bf16[64,4,256]{2,0,1:T(8,128)(2,1)}, bf16[64,4,256]{2,0,1:T(8,128)(2,1)S(1)}, u32[]{:S(2)}) copy-start(bf16[64,4,256]{2,0,1:T(8,128)(2,1)S(1)} %all-to-all-done.1) | copy-start | bytes 393220
  21.2 16.7 %all-to-all-start = ((bf16[64,4,1024]{2,0,1:T(8,128)(2,1)}), bf16[64,4,1024]{2,0,1:T(8,128)(2,1)S(1)}, u32[]{:S(2)}, u32[]{:S(2)}) async-start(bf16[64,4,1024]{2,0,1:T(8,128)(2,1)} %bitcast.85), calls=%async_computation | async-start | bytes 1048576 | tf_op jit(solution)/shard_map/all_to_all | solution.py:53
  24.7 28.1 %all-gather.2.cloned.1.call-start = ((), (), s32[]{:S(2)}) async-start(), calls=%async_computation.2 | async-start | bytes 1179648 | tf_op jit(solution)/shard_map/all_gather | solution.py:163
  25.4 183.1 %all-reduce.3.cloned.1.call-start = ((), (), s32[]{:S(2)}) async-start(), calls=%async_computation.3 | async-start | bytes 1310720 | tf_op jit(solution)/shard_map/psum | solution.py:171
  38.3 3.3 %copy-start.4 = (bf16[256,2,4,128]{3,2,1,0:T(4,128)(2,1)}, bf16[256,2,4,128]{3,2,1,0:T(4,128)(2,1)S(1)}, u32[]{:S(2)}) copy-start(bf16[256,2,4,128]{3,2,1,0:T(4,128)(2,1)S(1)} %reshape.230) | copy-start | bytes 1572868
  46.5 10.8 %copy-start.2 = (f32[2,4,256,256]{3,2,1,0:T(8,128)}, f32[2,4,256,256]{3,2,1,0:T(8,128)S(1)}, u32[]{:S(2)}) copy-start(f32[2,4,256,256]{3,2,1,0:T(8,128)S(1)} %copy.94) | copy-start | bytes 6291460
  46.5 10.8 %copy-start.9 = (s32[16]{0:T(128)S(1)}, s32[16]{0:T(128)}, u32[]{:S(2)}) copy-start(s32[16]{0:T(128)} %param.15) | copy-start | bytes 196
  59.5 2.6 %copy-start.6 = (bf16[2,1024,256]{2,1,0:T(8,128)(2,1)S(1)}, bf16[2,1024,256]{2,1,0:T(8,128)(2,1)}, u32[]{:S(2)}) copy-start(bf16[2,1024,256]{2,1,0:T(8,128)(2,1)} %get-tuple-element.788) | copy-start | bytes 3145732 | tf_op jit(solution)/shard_map/while/body/eval_jaxpr/cond
  68.4 2.6 %copy-start.6 = (bf16[2,1024,256]{2,1,0:T(8,128)(2,1)S(1)}, bf16[2,1024,256]{2,1,0:T(8,128)(2,1)}, u32[]{:S(2)}) copy-start(bf16[2,1024,256]{2,1,0:T(8,128)(2,1)} %get-tuple-element.788) | copy-start | bytes 3145732 | tf_op jit(solution)/shard_map/while/body/eval_jaxpr/cond
  77.3 2.6 %copy-start.6 = (bf16[2,1024,256]{2,1,0:T(8,128)(2,1)S(1)}, bf16[2,1024,256]{2,1,0:T(8,128)(2,1)}, u32[]{:S(2)}) copy-start(bf16[2,1024,256]{2,1,0:T(8,128)(2,1)} %get-tuple-element.788) | copy-start | bytes 3145732 | tf_op jit(solution)/shard_map/while/body/eval_jaxpr/cond
  90.4 2.9 %copy-start.1 = (bf16[2,1024,256]{1,2,0:T(8,128)(2,1)S(1)}, bf16[2,1024,256]{1,2,0:T(8,128)(2,1)}, u32[]{:S(2)}) copy-start(bf16[2,1024,256]{1,2,0:T(8,128)(2,1)} %get-tuple-element.813) | copy-start | bytes 3145732 | tf_op jit(solution)/shard_map/while/body/eval_jaxpr/cond
  90.4 2.9 %copy-start.3 = (pred[1024,512]{0,1:T(8,128)(4,1)S(1)}, pred[1024,512]{0,1:T(8,128)(4,1)}, u32[]{:S(2)}) copy-start(pred[1024,512]{0,1:T(8,128)(4,1)} %get-tuple-element.805) | copy-start | bytes 1572868 | tf_op jit(solution)/shard_map/while/body/eval_jaxpr/cond
  103.8 2.9 %copy-start.1 = (bf16[2,1024,256]{1,2,0:T(8,128)(2,1)S(1)}, bf16[2,1024,256]{1,2,0:T(8,128)(2,1)}, u32[]{:S(2)}) copy-start(bf16[2,1024,256]{1,2,0:T(8,128)(2,1)} %get-tuple-element.813) | copy-start | bytes 3145732 | tf_op jit(solution)/shard_map/while/body/eval_jaxpr/cond
  103.8 2.9 %copy-start.3 = (pred[1024,512]{0,1:T(8,128)(4,1)S(1)}, pred[1024,512]{0,1:T(8,128)(4,1)}, u32[]{:S(2)}) copy-start(pred[1024,512]{0,1:T(8,128)(4,1)} %get-tuple-element.805) | copy-start | bytes 1572868 | tf_op jit(solution)/shard_map/while/body/eval_jaxpr/cond
  117.3 2.9 %copy-start.1 = (bf16[2,1024,256]{1,2,0:T(8,128)(2,1)S(1)}, bf16[2,1024,256]{1,2,0:T(8,128)(2,1)}, u32[]{:S(2)}) copy-start(bf16[2,1024,256]{1,2,0:T(8,128)(2,1)} %get-tuple-element.813) | copy-start | bytes 3145732 | tf_op jit(solution)/shard_map/while/body/eval_jaxpr/cond
  117.3 2.9 %copy-start.3 = (pred[1024,512]{0,1:T(8,128)(4,1)S(1)}, pred[1024,512]{0,1:T(8,128)(4,1)}, u32[]{:S(2)}) copy-start(pred[1024,512]{0,1:T(8,128)(4,1)} %get-tuple-element.805) | copy-start | bytes 1572868 | tf_op jit(solution)/shard_map/while/body/eval_jaxpr/cond
  129.4 5.2 %copy-start.7 = (f32[2,128,128]{2,1,0:T(8,128)}, f32[2,128,128]{2,1,0:T(8,128)S(1)}, u32[]{:S(2)}) copy-start(f32[2,128,128]{2,1,0:T(8,128)S(1)} %get-tuple-element.842) | copy-start | bytes 393220
  129.4 4.1 %copy-start.5 = (bf16[256,2,4,128]{3,2,1,0:T(4,128)(2,1)S(1)}, bf16[256,2,4,128]{3,2,1,0:T(4,128)(2,1)}, u32[]{:S(2)}) copy-start(bf16[256,2,4,128]{3,2,1,0:T(4,128)(2,1)} %copy-done.4) | copy-start | bytes 1572868
Sparse Core Ops, SparseCore 0:
  28.0 24.7 all-gather.1
  135.7 72.8 all-reduce.2
where the time goes:
time: 220 us; the launch traced here: 219 us
  waiting for transfers between devices  91.3 us (42%)
  matrix products  42.5 us (19%)
  other arithmetic  36.6 us (17%)
  local copies, waits for them, and re-layouts  18.5 us (8%)
  between operations  14.3 us (6%)
  starting transfers between devices  9.9 us (4%)
  loops' own time  5.95 us (3%)
    psum x1, waiting for transfers between devices, per_device(): lax.psum((query_weight_grad, key_weight_grad), 'seq')  73 us
    dot_general x6, matrix products, teacher(): jnp.einsum('vrd,vwd->vrw', query_flat, key_slab, preferred_element_type=j...  10.9 us
    all_to_all x1, waiting for transfers between devices, per_device(): lax.all_to_all(queries, 'head', split_axis=1, concat_axis=0, tiled=True)  10.6 us
    unnamed x19, local copies, waits for them, and re-layouts  9.04 us
    dot_general x6, matrix products, key_features(): jnp.einsum('vwd,vde->vwe', key_slab.astype(jnp.float32), key_map, precisi...  8.25 us
    reduce_or x4, other arithmetic, grads_step(): jnp.any(visible)  7.75 us
    dot_general x3, matrix products, grads_compute_live(): jnp.einsum('vrf,vwf->vrw', phi_query_b, phi_key_b, preferred_element_type...  7.47 us
    all_to_all x1, starting transfers between devices, per_device(): lax.all_to_all(keys, 'head', split_axis=1, concat_axis=0, tiled=True)  6.35 us
  transfers between devices with their start and end apart: 4, of which 4 were waited for; matrix products, arithmetic and copies ran while one was open for 7% of the time, Pallas kernels for 0%

commit v1 on v0

--- a/solution.py
+++ b/solution.py
@@ -8,6 +8,28 @@
 BLK = 128
 HIGHEST = lax.Precision.HIGHEST
 NEG_FLOOR = -1e30
+
+
+def cut_along(x, dim, length):
+    before, after = (x.shape[:dim], x.shape[dim + 1 :])
+    return jnp.moveaxis(x.reshape(*before, length, -1, *after), dim, 0)
+
+
+def joined_along(blocks, dim):
+    blocks = jnp.moveaxis(blocks, 0, dim)
+    shape = blocks.shape
+    return blocks.reshape(*shape[:dim], shape[dim] * shape[dim + 1], *shape[dim + 2 :])
+
+
+def swapped_with_each(value, axis, split_dim, concat_dim):
+    peers, place = (lax.axis_size(axis), lax.axis_index(axis))
+    blocks = cut_along(value, split_dim, peers)
+    outs = [blocks[place]]
+    for step in range(1, peers):
+        sent = blocks[place ^ step]
+        outs.append(lax.ppermute(sent, axis, [(i, i ^ step) for i in range(peers)]))
+    blocks = jnp.stack(outs)[place ^ jnp.arange(peers)]
+    return joined_along(blocks, concat_dim)
 
 
 def softmax_pair(logits):
@@ -51,7 +73,7 @@
 def per_device(queries, keys, block_pos, query_map, key_map):
     local_q, local_k = (
         lax.all_to_all(queries, "head", split_axis=1, concat_axis=0, tiled=True),
-        lax.all_to_all(keys, "head", split_axis=1, concat_axis=0, tiled=True),
+        swapped_with_each(keys, "head", 1, 0),
     )
     seq_count = lax.axis_size("seq")
     seq_rank = lax.axis_index("seq")

time: 220 us -> 214 us (0.973)
  waiting for transfers between devices: 91.3 us -> 87.3 us
    all_to_all x1 -> x0, starting transfers between devices: 6.35 us -> none  [per_device(): lax.all_to_all(keys, 'head', split_axis=1, concat_axis=0, tiled=True)]
    ppermute x0 -> x3, starting transfers between devices: none -> 5.71 us  [swapped_with_each(): outs.append(lax.ppermute(sent, axis, [(i, i ^ step) for i in range(peers)]))]
    all_to_all x1 -> x0, waiting for transfers between devices: 4.2 us -> none  [per_device(): lax.all_to_all(keys, 'head', split_axis=1, concat_axis=0, tiled=True)]
    all_gather x1 -> x0, local copies, waits for them, and re-layouts: 2.28 us -> none  [per_device(): lax.all_gather(local_k, 'seq', axis=0, tiled=True)]
    unnamed x19 -> x23, local copies, waits for them, and re-layouts: 9.04 us -> 8.16 us
  transfers between devices with their start and end apart: 4 -> 6, of which waited for: 4 -> 3; matrix products, arithmetic and copies ran while one was open for 7% -> 7% of each run, Pallas kernels for 0% -> 0%
where the time goes in v1:
time: 214 us; the launch traced here: 213 us
  waiting for transfers between devices  87.3 us (41%)
  matrix products  42.5 us (20%)
  other arithmetic  35.9 us (17%)
  local copies, waits for them, and re-layouts  16.4 us (8%)
  between operations  14.4 us (7%)
  starting transfers between devices  10.8 us (5%)
  loops' own time  5.95 us (3%)
    psum x1, waiting for transfers between devices, per_device(): lax.psum((query_weight_grad, key_weight_grad), 'seq')  73 us
    all_to_all x1, waiting for transfers between devices, per_device(): lax.all_to_all(queries, 'head', split_axis=1, concat_axis=0, tiled=True)  11.9 us
    dot_general x6, matrix products, teacher(): jnp.einsum('vrd,vwd->vrw', query_flat, key_slab, preferred_element_type=j...  10.9 us
    dot_general x6, matrix products, key_features(): jnp.einsum('vwd,vde->vwe', key_slab.astype(jnp.float32), key_map, precisi...  8.25 us
    unnamed x23, local copies, waits for them, and re-layouts  8.16 us
    reduce_or x4, other arithmetic, grads_step(): jnp.any(visible)  7.75 us
    dot_general x3, matrix products, grads_compute_live(): jnp.einsum('vrf,vwf->vrw', phi_query_b, phi_key_b, preferred_element_type...  7.47 us
    ppermute x3, starting transfers between devices, swapped_with_each(): outs.append(lax.ppermute(sent, axis, [(i, i ^ step) for i in range(peers)]))  5.71 us
  transfers between devices with their start and end apart: 6, of which 3 were waited for; matrix products, arithmetic and copies ran while one was open for 7% of the time, Pallas kernels for 0%

profile of v1, /device:TPU:0, one launch (start us, length us, event | category | flops | bytes accessed | tf_op | source)
XLA Modules:
  0.0 213.3 jit_solution(18292937560824877490)
XLA Ops:
  8.6 3.1 %collective-permute-start = (bf16[64,256]{1,0:T(8,128)(2,1)S(1)}, bf16[64,256]{1,0:T(8,128)(2,1)S(1)}, u32[]{:S(2)}, u32[]{:S(2)}) collective-permute-start(bf16[64,256]{1,0:T(8,128)(2,1)S(1)} %bitcast.125), channel_id=1, source_target_pairs={{0,1},{1,0},{2,3},{3,2},{4,5},{5,4},{6,7},{7,6},{8,9},{9,8},{10,11... | collective-permute-start | bytes 98312 | tf_op jit(solution)/shard_map/ppermute | solution.py:30
  11.7 2.6 %collective-permute-start.1 = (bf16[64,256]{1,0:T(8,128)(2,1)S(1)}, bf16[64,256]{1,0:T(8,128)(2,1)S(1)}, u32[]{:S(2)}, u32[]{:S(2)}) collective-permute-start(bf16[64,256]{1,0:T(8,128)(2,1)S(1)} %bitcast.126), channel_id=1, source_target_pairs={{0,2},{1,3},{2,0},{3,1},{4,6},{5,7},{6,4},{7,5},{8,10},{9,11},{10,... | collective-permute-start | bytes 98312 | tf_op jit(solution)/shard_map/ppermute | solution.py:30
  14.3 1.9 copy.113
  16.2 5.1 %all-to-all-start = ((bf16[64,4,1024]{2,0,1:T(8,128)(2,1)}), bf16[64,4,1024]{2,0,1:T(8,128)(2,1)S(1)}, u32[]{:S(2)}, u32[]{:S(2)}) async-start(bf16[64,4,1024]{2,0,1:T(8,128)(2,1)} %bitcast.93), calls=%async_computation | async-start | bytes 1048576 | tf_op jit(solution)/shard_map/all_to_all | solution.py:75
  23.0 11.9 %all-to-all-done = bf16[64,4,1024]{2,0,1:T(8,128)(2,1)S(1)} async-done(((bf16[64,4,1024]{2,0,1:T(8,128)(2,1)}), bf16[64,4,1024]{2,0,1:T(8,128)(2,1)S(1)}, u32[]{:S(2)}, u32[]{:S(2)}) %all-to-all-start) | async-done | bytes 524320 | tf_op jit(solution)/shard_map/all_to_all | solution.py:75
  38.6 3.0 %pad_maximum_fusion.3 = f32[2,4,256,256]{2,3,1,0:T(8,128)} fusion(f32[2,4,256,128]{2,3,1,0:T(8,128)} %fusion.93, f32[2,4,256,128]{2,3,1,0:T(8,128)} %fusion.95), kind=kLoop, calls=%fused_computation.127 | loop fusion | flops 524288 | bytes 4194304 | tf_op jit(solution)/shard_map/concatenate | solution.py:36
  41.6 2.0 copy.72
  44.8 2.3 %copy.78 = bf16[2,1024,256]{1,2,0:T(8,128)(2,1)} copy(bf16[2,1024,256]{2,1,0:T(8,128)(2,1)} %bitcast_convert_fusion) | data formatting | bytes 2097152
  47.1 2.4 %all-gather.2.cloned.1.call-done = bf16[2048,256]{0,1:T(8,128)(2,1)} async-done(((bf16[256,256]{0,1:T(8,128)(2,1)}), bf16[2048,256]{0,1:T(8,128)(2,1)}) %all-gather.2.cloned.1.call-update) | async-done | bytes 1048592 | tf_op jit(solution)/shard_map/all_gather | solution.py:185
  49.5 2.3 %copy.74 = bf16[2,2048,128]{2,1,0:T(8,128)(2,1)} copy(bf16[2,2048,128]{1,2,0:T(8,128)(2,1)} %bitcast.117) | data formatting | bytes 2097152
  51.8 28.7 %while.40 = (s32[]{:T(128)}, f32[2,1024]{1,0:T(2,128)S(1)}, f32[2,1024]{1,0:T(2,128)S(1)}, f32[2,1024]{1,0:T(2,128)S(1)}, s32[16]{0:T(128)S(1)}, /*index=5*/bf16...) while((s32[]{:T(128)}, f32[2,1024]{1,0:T(2,128)S(1)}, ...), condition=%wide.region_17.18_spmd.clone, body=%wide.region_5.17_spmd.clone.sunk | while | flops 1021495552 | bytes 21834140 | solution.py:70
  53.9 6.8 %conditional.6 = ((f32[2,1024]{1,0:T(2,128)S(1)}, f32[2,1024]{1,0:T(2,128)S(1)}, f32[2,1024]{1,0:T(2,128)S(1)})) conditional(s32[]{:T(128)} %convert_element_type.44, (f32[2,1024]{1,0:T(2,128)S(1)}, f32[2,1024]{1,0:T(2,128)S(1)}, f32[2,1024]{1,0:T(2,128)S(1)}) %tuple.151, (pred[1024,512]{0,1:T(8,128)(4,1)S(1)}, s32[]{:T(128)}, ...), branch_computations={%region_8.8_spmd, %region_9.16_spmd} | conditional | flops 1019351296 | bytes 21258342 | solution.py:138
  53.9 1.4 fusion.20
  57.6 2.0 fusion.11
  62.8 6.8 %conditional.6 = ((f32[2,1024]{1,0:T(2,128)S(1)}, f32[2,1024]{1,0:T(2,128)S(1)}, f32[2,1024]{1,0:T(2,128)S(1)})) conditional(s32[]{:T(128)} %convert_element_type.44, (f32[2,1024]{1,0:T(2,128)S(1)}, f32[2,1024]{1,0:T(2,128)S(1)}, f32[2,1024]{1,0:T(2,128)S(1)}) %tuple.151, (pred[1024,512]{0,1:T(8,128)(4,1)S(1)}, s32[]{:T(128)}, ...), branch_computations={%region_8.8_spmd, %region_9.16_spmd} | conditional | flops 1019351296 | bytes 21258342 | solution.py:138
  62.8 1.4 fusion.20
  66.4 2.0 fusion.11
  71.6 6.8 %conditional.6 = ((f32[2,1024]{1,0:T(2,128)S(1)}, f32[2,1024]{1,0:T(2,128)S(1)}, f32[2,1024]{1,0:T(2,128)S(1)})) conditional(s32[]{:T(128)} %convert_element_type.44, (f32[2,1024]{1,0:T(2,128)S(1)}, f32[2,1024]{1,0:T(2,128)S(1)}, f32[2,1024]{1,0:T(2,128)S(1)}) %tuple.151, (pred[1024,512]{0,1:T(8,128)(4,1)S(1)}, s32[]{:T(128)}, ...), branch_computations={%region_8.8_spmd, %region_9.16_spmd} | conditional | flops 1019351296 | bytes 21258342 | solution.py:138
  71.7 1.4 fusion.20
  75.3 2.0 fusion.11
  80.7 43.1 %while.41 = (s32[]{:T(128)}, f32[2,1024,256]{2,1,0:T(8,128)S(1)}, f32[2,128,128]{2,1,0:T(8,128)S(1)}, s32[16]{0:T(128)S(1)}, f32[2,1024]{1,0:T(2,128)S(1)}, /*in...) while((s32[]{:T(128)}, f32[2,1024,256]{2,1,0:T(8,128)S(1)}, ...), condition=%wide.region_29.30_spmd.clone, body=%wide.region_18.29_spmd.clone.sunk | while | flops 2299869440 | bytes 40643016 | solution.py:70
  80.9 1.9 fusion.131
  83.4 10.8 %conditional.7 = ((f32[2,1024,256]{2,1,0:T(8,128)S(1)}, f32[2,128,128]{2,1,0:T(8,128)S(1)})) conditional(s32[]{:T(128)} %convert_element_type.45, (f32[2,1024,256]{2,1,0:T(8,128)S(1)}, f32[2,128,128]{2,1,0:T(8,128)S(1)}) %tuple.157, (pred[1024,512]{0,1:T(8,128)(4,1)}, f32[2,1024]{1,0:T(2,128)S(1)}, s32[]{:T(128)}, ...), branch_computations={%region_21.21_spmd, %region_22.28_spmd} | conditional | flops 2297725184 | bytes 40067196 | solution.py:170
  83.4 1.3 fusion.51
  85.9 1.7 fusion.53
  87.6 2.5 %fusion.35 = bf16[2,1024,512]{1,2,0:T(8,128)(2,1)S(1)} fusion(f32[2,512,1024]{2,1,0:T(8,128)S(1)} %fusion.53, bf16[2,1024,256]{1,2,0:T(8,128)(2,1)S(1)} %copy-done.1, f32[2,1024]{1,0:T(2,128)S(1)} %get-tuple-element.811, f32[2,1024]{1,0:T(2,128)S(1)} %get-tuple-element.810, f32[2,1024]{1,0:T(2,128)S(1)} %broadcast_divide_fusion.2, ...), kind=kOutput, calls=%fused_computation.41 | convolution fusion | flops 548405248 | bytes 8413184 | tf_op jit(solution)/shard_map/while/body/eval_jaxpr/cond/branch_1_fun/vrf,vwf->vrw/dot_general | solution.py:151
  90.9 1.4 convolution_add_fusion
  92.6 1.6 convolution_add_fusion.1
  94.3 1.9 fusion.131
  96.8 10.8 %conditional.7 = ((f32[2,1024,256]{2,1,0:T(8,128)S(1)}, f32[2,128,128]{2,1,0:T(8,128)S(1)})) conditional(s32[]{:T(128)} %convert_element_type.45, (f32[2,1024,256]{2,1,0:T(8,128)S(1)}, f32[2,128,128]{2,1,0:T(8,128)S(1)}) %tuple.157, (pred[1024,512]{0,1:T(8,128)(4,1)}, f32[2,1024]{1,0:T(2,128)S(1)}, s32[]{:T(128)}, ...), branch_computations={%region_21.21_spmd, %region_22.28_spmd} | conditional | flops 2297725184 | bytes 40067196 | solution.py:170
  96.9 1.3 fusion.51
  99.4 1.7 fusion.53
  101.1 2.5 %fusion.35 = bf16[2,1024,512]{1,2,0:T(8,128)(2,1)S(1)} fusion(f32[2,512,1024]{2,1,0:T(8,128)S(1)} %fusion.53, bf16[2,1024,256]{1,2,0:T(8,128)(2,1)S(1)} %copy-done.1, f32[2,1024]{1,0:T(2,128)S(1)} %get-tuple-element.811, f32[2,1024]{1,0:T(2,128)S(1)} %get-tuple-element.810, f32[2,1024]{1,0:T(2,128)S(1)} %broadcast_divide_fusion.2, ...), kind=kOutput, calls=%fused_computation.41 | convolution fusion | flops 548405248 | bytes 8413184 | tf_op jit(solution)/shard_map/while/body/eval_jaxpr/cond/branch_1_fun/vrf,vwf->vrw/dot_general | solution.py:151
  104.3 1.4 convolution_add_fusion
  106.0 1.6 convolution_add_fusion.1
  107.8 1.9 fusion.131
  110.3 10.8 %conditional.7 = ((f32[2,1024,256]{2,1,0:T(8,128)S(1)}, f32[2,128,128]{2,1,0:T(8,128)S(1)})) conditional(s32[]{:T(128)} %convert_element_type.45, (f32[2,1024,256]{2,1,0:T(8,128)S(1)}, f32[2,128,128]{2,1,0:T(8,128)S(1)}) %tuple.157, (pred[1024,512]{0,1:T(8,128)(4,1)}, f32[2,1024]{1,0:T(2,128)S(1)}, s32[]{:T(128)}, ...), branch_computations={%region_21.21_spmd, %region_22.28_spmd} | conditional | flops 2297725184 | bytes 40067196 | solution.py:170
  110.3 1.3 fusion.51
  112.9 1.7 fusion.53
  114.6 2.5 %fusion.35 = bf16[2,1024,512]{1,2,0:T(8,128)(2,1)S(1)} fusion(f32[2,512,1024]{2,1,0:T(8,128)S(1)} %fusion.53, bf16[2,1024,256]{1,2,0:T(8,128)(2,1)S(1)} %copy-done.1, f32[2,1024]{1,0:T(2,128)S(1)} %get-tuple-element.811, f32[2,1024]{1,0:T(2,128)S(1)} %get-tuple-element.810, f32[2,1024]{1,0:T(2,128)S(1)} %broadcast_divide_fusion.2, ...), kind=kOutput, calls=%fused_computation.41 | convolution fusion | flops 548405248 | bytes 8413184 | tf_op jit(solution)/shard_map/while/body/eval_jaxpr/cond/branch_1_fun/vrf,vwf->vrw/dot_general | solution.py:151
  117.8 1.4 convolution_add_fusion
  119.5 1.6 convolution_add_fusion.1
  121.3 1.9 fusion.131
  123.8 2.0 fusion.86
  125.8 2.1 fusion.84
  130.0 73.0 %all-reduce.3.cloned.1.call-done = (f32[8,128,128]{2,1,0:T(8,128)}, f32[2,128,128]{2,1,0:T(8,128)}) async-done(((f32[8,128,128]{2,1,0:T(8,128)}, f32[2,128,128]{2,1,0:T(8,128)}), (f32[8,128,128]{2,1,0:T(8,128)}, f32[2,128,128]{2,1,0:T(8,128)})) %all-reduce.3.cloned.1.call-update) | async-done | bytes 655376 | tf_op jit(solution)/shard_map/psum | solution.py:193
  203.0 1.9 copy.161
  204.9 1.6 copy.162
  (167 shorter events, 32.6 us)
Async XLA Ops:
  7.2 28.2 %copy-start = (f32[8,128,128]{2,1,0:T(8,128)S(1)}, f32[8,128,128]{2,1,0:T(8,128)}, u32[]{:S(2)}) copy-start(f32[8,128,128]{2,1,0:T(8,128)} %param.16) | copy-start | bytes 1572868
  7.2 15.6 %copy-start.8 = (f32[2,128,128]{2,1,0:T(8,128)S(1)}, f32[2,128,128]{2,1,0:T(8,128)}, u32[]{:S(2)}) copy-start(f32[2,128,128]{2,1,0:T(8,128)} %param.17) | copy-start | bytes 393220
  7.2 15.7 %copy-start.9 = (s32[16]{0:T(128)S(1)}, s32[16]{0:T(128)}, u32[]{:S(2)}) copy-start(s32[16]{0:T(128)} %param.15) | copy-start | bytes 196
  8.6 12.7 %collective-permute-start = (bf16[64,256]{1,0:T(8,128)(2,1)S(1)}, bf16[64,256]{1,0:T(8,128)(2,1)S(1)}, u32[]{:S(2)}, u32[]{:S(2)}) collective-permute-start(bf16[64,256]{1,0:T(8,128)(2,1)S(1)} %bitcast.125), channel_id=1, source_target_pairs={{0,1},{1,0},{2,3},{3,2},{4,5},{5,4},{6,7},{7,6},{8,9},{9,8},{10,11... | collective-permute-start | bytes 98312 | tf_op jit(solution)/shard_map/ppermute | solution.py:30
  11.7 9.6 %collective-permute-start.1 = (bf16[64,256]{1,0:T(8,128)(2,1)S(1)}, bf16[64,256]{1,0:T(8,128)(2,1)S(1)}, u32[]{:S(2)}, u32[]{:S(2)}) collective-permute-start(bf16[64,256]{1,0:T(8,128)(2,1)S(1)} %bitcast.126), channel_id=1, source_target_pairs={{0,2},{1,3},{2,0},{3,1},{4,6},{5,7},{6,4},{7,5},{8,10},{9,11},{10,... | collective-permute-start | bytes 98312 | tf_op jit(solution)/shard_map/ppermute | solution.py:30
  14.3 7.0 %collective-permute-start.2 = (bf16[64,256]{1,0:T(8,128)(2,1)S(1)}, bf16[64,256]{1,0:T(8,128)(2,1)S(1)}, u32[]{:S(2)}, u32[]{:S(2)}) collective-permute-start(bf16[64,256]{1,0:T(8,128)(2,1)S(1)} %bitcast.127), channel_id=1, source_target_pairs={{0,3},{1,2},{2,1},{3,0},{4,7},{5,6},{6,5},{7,4},{8,11},{9,10},{10,... | collective-permute-start | bytes 98312 | tf_op jit(solution)/shard_map/ppermute | solution.py:30
  16.2 18.7 %all-to-all-start = ((bf16[64,4,1024]{2,0,1:T(8,128)(2,1)}), bf16[64,4,1024]{2,0,1:T(8,128)(2,1)S(1)}, u32[]{:S(2)}, u32[]{:S(2)}) async-start(bf16[64,4,1024]{2,0,1:T(8,128)(2,1)} %bitcast.93), calls=%async_computation | async-start | bytes 1048576 | tf_op jit(solution)/shard_map/all_to_all | solution.py:75
  21.3 28.2 %all-gather.2.cloned.1.call-start = ((), (), s32[]{:S(2)}) async-start(), calls=%async_computation.1 | async-start | bytes 1179648 | tf_op jit(solution)/shard_map/all_gather | solution.py:185
  22.7 180.3 %all-reduce.3.cloned.1.call-start = ((), (), s32[]{:S(2)}) async-start(), calls=%async_computation.2 | async-start | bytes 1310720 | tf_op jit(solution)/shard_map/psum | solution.py:193
  35.3 3.3 %copy-start.4 = (bf16[256,2,4,128]{3,2,1,0:T(4,128)(2,1)}, bf16[256,2,4,128]{3,2,1,0:T(4,128)(2,1)S(1)}, u32[]{:S(2)}) copy-start(bf16[256,2,4,128]{3,2,1,0:T(4,128)(2,1)S(1)} %reshape.256) | copy-start | bytes 1572868
  43.6 8.2 %copy-start.2 = (f32[2,4,256,256]{3,2,1,0:T(8,128)}, f32[2,4,256,256]{3,2,1,0:T(8,128)S(1)}, u32[]{:S(2)}) copy-start(f32[2,4,256,256]{3,2,1,0:T(8,128)S(1)} %copy.72) | copy-start | bytes 6291460
  53.9 2.6 %copy-start.6 = (bf16[2,1024,256]{2,1,0:T(8,128)(2,1)S(1)}, bf16[2,1024,256]{2,1,0:T(8,128)(2,1)}, u32[]{:S(2)}) copy-start(bf16[2,1024,256]{2,1,0:T(8,128)(2,1)} %get-tuple-element.788) | copy-start | bytes 3145732 | tf_op jit(solution)/shard_map/while/body/eval_jaxpr/cond
  62.8 2.6 %copy-start.6 = (bf16[2,1024,256]{2,1,0:T(8,128)(2,1)S(1)}, bf16[2,1024,256]{2,1,0:T(8,128)(2,1)}, u32[]{:S(2)}) copy-start(bf16[2,1024,256]{2,1,0:T(8,128)(2,1)} %get-tuple-element.788) | copy-start | bytes 3145732 | tf_op jit(solution)/shard_map/while/body/eval_jaxpr/cond
  71.7 2.6 %copy-start.6 = (bf16[2,1024,256]{2,1,0:T(8,128)(2,1)S(1)}, bf16[2,1024,256]{2,1,0:T(8,128)(2,1)}, u32[]{:S(2)}) copy-start(bf16[2,1024,256]{2,1,0:T(8,128)(2,1)} %get-tuple-element.788) | copy-start | bytes 3145732 | tf_op jit(solution)/shard_map/while/body/eval_jaxpr/cond
  84.8 2.9 %copy-start.1 = (bf16[2,1024,256]{1,2,0:T(8,128)(2,1)S(1)}, bf16[2,1024,256]{1,2,0:T(8,128)(2,1)}, u32[]{:S(2)}) copy-start(bf16[2,1024,256]{1,2,0:T(8,128)(2,1)} %get-tuple-element.813) | copy-start | bytes 3145732 | tf_op jit(solution)/shard_map/while/body/eval_jaxpr/cond
  84.8 2.9 %copy-start.3 = (pred[1024,512]{0,1:T(8,128)(4,1)S(1)}, pred[1024,512]{0,1:T(8,128)(4,1)}, u32[]{:S(2)}) copy-start(pred[1024,512]{0,1:T(8,128)(4,1)} %get-tuple-element.805) | copy-start | bytes 1572868 | tf_op jit(solution)/shard_map/while/body/eval_jaxpr/cond
  98.2 2.9 %copy-start.1 = (bf16[2,1024,256]{1,2,0:T(8,128)(2,1)S(1)}, bf16[2,1024,256]{1,2,0:T(8,128)(2,1)}, u32[]{:S(2)}) copy-start(bf16[2,1024,256]{1,2,0:T(8,128)(2,1)} %get-tuple-element.813) | copy-start | bytes 3145732 | tf_op jit(solution)/shard_map/while/body/eval_jaxpr/cond
  98.2 2.9 %copy-start.3 = (pred[1024,512]{0,1:T(8,128)(4,1)S(1)}, pred[1024,512]{0,1:T(8,128)(4,1)}, u32[]{:S(2)}) copy-start(pred[1024,512]{0,1:T(8,128)(4,1)} %get-tuple-element.805) | copy-start | bytes 1572868 | tf_op jit(solution)/shard_map/while/body/eval_jaxpr/cond
  111.7 2.9 %copy-start.1 = (bf16[2,1024,256]{1,2,0:T(8,128)(2,1)S(1)}, bf16[2,1024,256]{1,2,0:T(8,128)(2,1)}, u32[]{:S(2)}) copy-start(bf16[2,1024,256]{1,2,0:T(8,128)(2,1)} %get-tuple-element.813) | copy-start | bytes 3145732 | tf_op jit(solution)/shard_map/while/body/eval_jaxpr/cond
  111.7 2.9 %copy-start.3 = (pred[1024,512]{0,1:T(8,128)(4,1)S(1)}, pred[1024,512]{0,1:T(8,128)(4,1)}, u32[]{:S(2)}) copy-start(pred[1024,512]{0,1:T(8,128)(4,1)} %get-tuple-element.805) | copy-start | bytes 1572868 | tf_op jit(solution)/shard_map/while/body/eval_jaxpr/cond
  123.8 5.2 %copy-start.7 = (f32[2,128,128]{2,1,0:T(8,128)}, f32[2,128,128]{2,1,0:T(8,128)S(1)}, u32[]{:S(2)}) copy-start(f32[2,128,128]{2,1,0:T(8,128)S(1)} %get-tuple-element.842) | copy-start | bytes 393220
  123.8 4.1 %copy-start.5 = (bf16[256,2,4,128]{3,2,1,0:T(4,128)(2,1)S(1)}, bf16[256,2,4,128]{3,2,1,0:T(4,128)(2,1)}, u32[]{:S(2)}) copy-start(bf16[256,2,4,128]{3,2,1,0:T(4,128)(2,1)} %copy-done.4) | copy-start | bytes 1572868
Sparse Core Ops, SparseCore 0:
  24.5 24.9 all-gather.1
  130.1 72.8 all-reduce.2
